TPU v7x, 128 devices: a whole 4x4x4 slice. The times are simulated.
128 devices in a mesh: dp: 16 (over y, x), head: 8 (over z, core).
Axes of the slice: x: 4, y: 4, z: 4, core: 2. Of those that a mesh axis runs over, the one named last changes fastest.
Arguments:
- slot_token_ids: int32 [128, 512], P('dp'), may hold values from 0 to 50264
- lengths: int32 [128], P('dp'), may hold values from 64 to 512, as said below
- labels: int32 [128], P('dp'), may hold values from 0 to 2
- optimizer_step_count: int32 [], replicated, may hold values from 2 to 20
- token_embedding_table: bfloat16 [50304, 1024], P('dp', 'head'), may hold values from -6 to 6
- positions: bfloat16 [512, 1024], replicated, may hold values from -4 to 4
- query_key_value_weight: bfloat16 [3, 1024, 1024], P(None, None, 'head'), may hold values from -0.1875 to 0.1875
- attention_output_weight: bfloat16 [1024, 1024], P('head'), may hold values from -0.8 to 0.8
- feedforward_input_weight: bfloat16 [1024, 4096], P(None, 'head'), may hold values from -0.1875 to 0.1875
- feedforward_output_weight: bfloat16 [4096, 1024], P('head'), may hold values from -0.09375 to 0.09375
- layer_norm_gains: float32 [3, 1024], replicated, may hold values from 0.5 to 1.5
- layer_norm_biases: float32 [3, 1024], replicated, may hold values from -2 to 2
- classifier: bfloat16 [3, 1024], replicated, may hold values from -0.75 to 0.75
- adapter_down_maps: float32 [2, 1024, 16], replicated, may hold values from -0.1875 to 0.1875
- adapter_up_maps: float32 [2, 16, 1024], P(None, None, 'head'), may hold values from -1.5 to 1.5
- down_first_moment: float32 [2, 1024, 16], P(None, 'dp'), may hold values from -0.0078125 to 0.0078125
- down_second_moment: float32 [2, 1024, 16], P(None, 'dp'), may hold values from 2.1972657e-08 to 9.1552735e-08
- up_first_moment: float32 [2, 16, 1024], P(None, None, ('head', 'dp')), may hold values from -0.0078125 to 0.0078125
- up_second_moment: float32 [2, 16, 1024], P(None, None, ('head', 'dp')), may hold values from 2.1972657e-08 to 9.1552735e-08
- down_privacy_noise: float32 [2, 1024, 16], P(None, 'dp'), may hold values from -6 to 6
- up_privacy_noise: float32 [2, 16, 1024], P(None, None, ('head', 'dp')), may hold values from -6 to 6
Outputs:
- loss: float32 [], replicated
- example_norms: float32 [128], P(('dp', 'head'))
- a_moment1: float32 [2, 1024, 16], P(None, 'dp')
- a_moment2: float32 [2, 1024, 16], P(None, 'dp')
- a_weight: float32 [2, 1024, 16], P(None, 'dp')
- b_moment1: float32 [2, 16, 1024], P(None, None, ('head', 'dp'))
- b_moment2: float32 [2, 16, 1024], P(None, None, ('head', 'dp'))
- b_weight: float32 [2, 16, 1024], P(None, None, ('head', 'dp'))
- lamb_norms: float32 [4, 2], replicated
Inputs may be any that keep to these rules, and one draw needn't show every extreme that they name: `lengths`: valid tokens of each example; some example has exactly 512.
All inputs are finite; a program needn't handle non-finite values.
Results may differ from a plain program's by a relative error of at most 0.0059.
Values may be sent and summed in bfloat16 or wider, within the bound.
No kernel may reach another device: no remote copies, remote signals or barrier semaphores. Data moves between devices by JAX's collectives and lax.ppermute only.
A program may use at most 256 MiB of HBM per device.

v0:
```python
import jax
import jax.numpy as jnp
from jax import lax
from jax.sharding import PartitionSpec as P

HDIM = 64
MICRO = 4
precise = lax.Precision.HIGHEST
adapter_scale = 2.0
clip_bound = 1.0
noise_mult = 0.6
smooth_rate = 0.1
beta_one = 0.9
beta_two = 0.999
adam_eps = 1e-06
decay_rate = 0.01
learn_rate = 0.25
norm_eps = 1e-05
contract_last = (((1,), (1,)), ((), ()))


def gelu_exact(inputs):
    return jax.nn.gelu(inputs, approximate=False)


def norm_rows(inputs, gain, bias):
    centre = inputs - jnp.mean(inputs, -1, keepdims=True)
    inv_std = lax.rsqrt(jnp.mean(centre * centre, -1, keepdims=True) + norm_eps)
    return (centre * inv_std * gain + bias, inv_std)


def norm_back(grad, normed, inv_std, gain, bias):
    x_hat = (normed - bias) / gain
    scaled = grad * gain
    return inv_std * (
        scaled
        - jnp.mean(scaled, -1, keepdims=True)
        - x_hat * jnp.mean(scaled * x_hat, -1, keepdims=True)
    )


def branch_add(partial_out, resid, gain, bias):
    total = lax.psum(partial_out, "head")
    return norm_rows(resid + total, gain, bias)


def masked_scores(query_h, key_h, valid_mask):
    scores = jnp.einsum(
        "eqhd,ekhd->ehqk", query_h, key_h, preferred_element_type=jnp.float32
    ) * HDIM ** (-0.5)
    return jnp.where(valid_mask[:, None, None, :], scores, -1e30)


def layer_forward(
    hidden_initial, valid_mask, length_float, class_label, frozen_params, adapter_reduced
):
    w_qkv, w_o, w_in, w_out, gains, biases, class_w = frozen_params
    down_pair, up_reduced = adapter_reduced
    example_count, sequence_length = valid_mask.shape
    width = hidden_initial.shape[1]
    local_w = w_o.shape[0]
    adapter_width = up_reduced.shape[1]
    shape4 = (example_count, sequence_length, local_w // HDIM, HDIM)
    hidden_reduced = hidden_initial.astype(jnp.bfloat16)
    adapter_activation = jnp.dot(
        hidden_reduced, down_pair, preferred_element_type=jnp.float32
    ).astype(jnp.bfloat16)
    query_low = (
        (
            jnp.dot(hidden_reduced, w_qkv[0], preferred_element_type=jnp.float32)
            + adapter_scale
            * jnp.dot(
                adapter_activation[:, :adapter_width],
                up_reduced[0],
                preferred_element_type=jnp.float32,
            )
        )
        .astype(jnp.bfloat16)
        .reshape(shape4)
    )
    key_low = (
        jnp.dot(hidden_reduced, w_qkv[1], preferred_element_type=jnp.float32)
        .astype(jnp.bfloat16)
        .reshape(shape4)
    )
    value_low = (
        (
            jnp.dot(hidden_reduced, w_qkv[2], preferred_element_type=jnp.float32)
            + adapter_scale
            * jnp.dot(
                adapter_activation[:, adapter_width:],
                up_reduced[1],
                preferred_element_type=jnp.float32,
            )
        )
        .astype(jnp.bfloat16)
        .reshape(shape4)
    )
    scores = masked_scores(query_low, key_low, valid_mask)
    row_top = jnp.max(scores, -1, keepdims=True)
    log_total = row_top + jnp.log(jnp.sum(jnp.exp(scores - row_top), -1, keepdims=True))
    attn_prob = jnp.exp(scores - log_total)
    context = (
        jnp.einsum(
            "ehqk,ekhd->eqhd",
            attn_prob.astype(jnp.bfloat16),
            value_low,
            preferred_element_type=jnp.float32,
        )
        .astype(jnp.bfloat16)
        .reshape(-1, local_w)
    )
    hidden_one, std_one = branch_add(
        jnp.dot(context, w_o, preferred_element_type=jnp.float32),
        hidden_initial,
        gains[1],
        biases[1],
    )
    ffn_pre = jnp.dot(hidden_one.astype(jnp.bfloat16), w_in, preferred_element_type=jnp.float32)
    ffn_part = jnp.dot(
        gelu_exact(ffn_pre).astype(jnp.bfloat16), w_out, preferred_element_type=jnp.float32
    )
    hidden_two, std_two = branch_add(ffn_part, hidden_one, gains[2], biases[2])
    valid_f = valid_mask.astype(jnp.float32)
    pooled = (
        jnp.sum(hidden_two.reshape(example_count, sequence_length, width) * valid_f[..., None], 1)
        / length_float[:, None]
    )
    logits = lax.dot_general(
        pooled.astype(jnp.bfloat16), class_w, contract_last, preferred_element_type=jnp.float32
    )
    log_prob = jax.nn.log_softmax(logits, -1)
    target = (1.0 - smooth_rate) * jax.nn.one_hot(
        class_label, class_w.shape[0], dtype=jnp.float32
    ) + smooth_rate / class_w.shape[0]
    losses = -jnp.sum(target * log_prob, -1)
    d_logit = jnp.exp(log_prob) - target
    d_pooled = jnp.dot(d_logit, class_w.astype(jnp.float32), precision=precise)
    d_two = (d_pooled[:, None, :] * (valid_f / length_float[:, None])[..., None]).reshape(-1, width)
    d_sum_two = norm_back(d_two, hidden_two, std_two, gains[2], biases[2])
    grad_act = lax.dot_general(
        d_sum_two.astype(jnp.bfloat16), w_out, contract_last, preferred_element_type=jnp.float32
    )
    d_pre = jax.vjp(gelu_exact, ffn_pre)[1](grad_act)[0].astype(jnp.bfloat16)
    back_part = lax.dot_general(d_pre, w_in, contract_last, preferred_element_type=jnp.float32)
    d_one = d_sum_two + lax.psum(back_part, "head")
    d_attn = norm_back(d_one, hidden_one, std_one, gains[1], biases[1]).astype(jnp.bfloat16)
    d_context = (
        lax.dot_general(d_attn, w_o, contract_last, preferred_element_type=jnp.float32)
        .astype(jnp.bfloat16)
        .reshape(shape4)
    )
    attn_prob = jnp.exp(masked_scores(query_low, key_low, valid_mask) - log_total)
    d_value = jnp.einsum(
        "ehqk,eqhd->ekhd",
        attn_prob.astype(jnp.bfloat16),
        d_context,
        preferred_element_type=jnp.float32,
    ).astype(jnp.bfloat16)
    d_prob = jnp.einsum("eqhd,ekhd->ehqk", d_context, value_low, preferred_element_type=jnp.float32)
    d_score = (attn_prob * (d_prob - jnp.sum(attn_prob * d_prob, -1, keepdims=True))).astype(
        jnp.bfloat16
    )
    d_query = (
        jnp.einsum("ehqk,ekhd->eqhd", d_score, key_low, preferred_element_type=jnp.float32)
        * HDIM ** (-0.5)
    ).astype(jnp.bfloat16)
    dq_rows = d_query.reshape(-1, local_w)
    dv_rows = d_value.reshape(-1, local_w)
    example_activation = adapter_activation.reshape(
        example_count, sequence_length, 2 * adapter_width
    )
    up_gradient = adapter_scale * jnp.stack(
        [
            jnp.einsum(
                "elr,eld->erd",
                example_activation[..., :adapter_width],
                dq_rows.reshape(example_count, sequence_length, local_w),
                preferred_element_type=jnp.float32,
            ),
            jnp.einsum(
                "elr,eld->erd",
                example_activation[..., adapter_width:],
                dv_rows.reshape(example_count, sequence_length, local_w),
                preferred_element_type=jnp.float32,
            ),
        ],
        1,
    )
    inner_portion = adapter_scale * jnp.concatenate(
        [
            lax.dot_general(
                dq_rows, up_reduced[0], contract_last, preferred_element_type=jnp.float32
            ),
            lax.dot_general(
                dv_rows, up_reduced[1], contract_last, preferred_element_type=jnp.float32
            ),
        ],
        1,
    )
    inner_full = lax.psum(inner_portion, "head")
    inner_sum = inner_full.astype(jnp.bfloat16)
    grad_both = jnp.einsum(
        "eld,elr->edr",
        hidden_reduced.reshape(example_count, sequence_length, width),
        inner_sum.reshape(example_count, sequence_length, 2 * adapter_width),
        preferred_element_type=jnp.float32,
    )
    down_gradient = jnp.stack([grad_both[..., :adapter_width], grad_both[..., adapter_width:]], 1)
    return (losses, down_gradient, up_gradient)


def apply_blocks(hidden_rows, lengths, labels, frozen_params, adapter_reduced, encoder_block):
    example_count, sequence_length, width = hidden_rows.shape
    valid_all = jnp.arange(sequence_length)[None, :] < lengths[:, None]
    loss_list, down_list, up_list = ([], [], [])
    for block_idx in range(example_count // encoder_block):
        first_ex = block_idx * encoder_block
        last_ex = first_ex + encoder_block
        losses, down_gradient, up_gradient = layer_forward(
            hidden_rows[first_ex:last_ex].reshape(-1, width),
            valid_all[first_ex:last_ex],
            lengths[first_ex:last_ex].astype(jnp.float32),
            labels[first_ex:last_ex],
            frozen_params,
            adapter_reduced,
        )
        loss_list.append(losses)
        down_list.append(down_gradient)
        up_list.append(up_gradient)
    return (
        jnp.concatenate(loss_list, 0),
        jnp.concatenate(down_list, 0),
        jnp.concatenate(up_list, 0),
    )


def lamb_direction(weight, grad, first, second, step_number):
    first_new = beta_one * first + (1.0 - beta_one) * grad
    second_new = beta_two * second + (1.0 - beta_two) * grad * grad
    direction = (
        first_new
        / (1.0 - jnp.power(beta_one, step_number))
        / (jnp.sqrt(second_new / (1.0 - jnp.power(beta_two, step_number))) + adam_eps)
        + decay_rate * weight
    )
    return (first_new, second_new, direction)


def per_device(
    slot_token_ids,
    lengths,
    labels,
    optimizer_step_count,
    token_embedding_table,
    positions,
    query_key_value_weight,
    attention_output_weight,
    feedforward_input_weight,
    feedforward_output_weight,
    layer_norm_gains,
    layer_norm_biases,
    classifier,
    adapter_down_maps,
    adapter_up_maps,
    down_first_moment,
    down_second_moment,
    up_first_moment,
    up_second_moment,
    down_privacy_noise,
    up_privacy_noise,
):
    n_head = lax.axis_size("head")
    dataset_size = lax.axis_size("dp")
    ex_dev, sequence_length = slot_token_ids.shape
    width = positions.shape[1]
    every_ids = lax.all_gather(slot_token_ids, "dp", axis=0, tiled=True).reshape(-1)
    vocab_local = token_embedding_table.shape[0]
    offset = lax.axis_index("dp") * vocab_local
    ids_here = every_ids - offset
    inside = (ids_here >= 0) & (ids_here < vocab_local)
    picked = jnp.take(token_embedding_table, jnp.clip(ids_here, 0, vocab_local - 1), axis=0)
    columns = lax.psum_scatter(
        jnp.where(inside[:, None], picked.astype(jnp.float32), 0.0).astype(jnp.bfloat16),
        "dp",
        scatter_dimension=0,
        tiled=True,
    )
    pos_f = positions.astype(jnp.float32)[None]
    down_reduced = adapter_down_maps.astype(jnp.bfloat16)
    down_pair = jnp.concatenate([down_reduced[0], down_reduced[1]], 1)
    micro_examples = ex_dev // MICRO
    own_share = ex_dev // n_head
    tokens = lax.all_gather(columns, "head", axis=1, tiled=True)
    hidden_all, unused_std = norm_rows(
        tokens.astype(jnp.float32).reshape(ex_dev, sequence_length, width) + pos_f,
        layer_norm_gains[0],
        layer_norm_biases[0],
    )
    frozen_params = (
        query_key_value_weight,
        attention_output_weight,
        feedforward_input_weight,
        feedforward_output_weight,
        layer_norm_gains,
        layer_norm_biases,
        classifier,
    )
    losses, grads_down, grads_up = apply_blocks(
        hidden_all,
        lengths,
        labels,
        frozen_params,
        (down_pair, adapter_up_maps.astype(jnp.bfloat16)),
        micro_examples,
    )
    part_sums = jnp.sum(grads_down * grads_down, (1, 2, 3)) / n_head + jnp.sum(
        grads_up * grads_up, (1, 2, 3)
    )
    arrived = lax.all_to_all(
        part_sums.reshape(n_head, own_share), "head", split_axis=0, concat_axis=0, tiled=True
    )
    example_norms = jnp.sqrt(jnp.sum(arrived, 0))
    own_factor = clip_bound / jnp.maximum(example_norms, clip_bound)
    factors = lax.all_gather(own_factor, "head", axis=0, tiled=True)
    sum_down = jnp.einsum("e,eabc->abc", factors, grads_down, precision=precise)
    sum_up = jnp.einsum("e,eabc->abc", factors, grads_up, precision=precise)
    loss_part = jnp.sum(losses) / n_head
    red_down, red_up = (
        lax.psum_scatter(sum_down, "dp", scatter_dimension=1, tiled=True),
        lax.psum_scatter(sum_up, "dp", scatter_dimension=2, tiled=True),
    )
    examples = ex_dev * dataset_size
    down_gradient = (red_down + noise_mult * clip_bound * down_privacy_noise) / examples
    up_gradient = (red_up + noise_mult * clip_bound * up_privacy_noise) / examples
    step_number = optimizer_step_count.astype(jnp.float32)
    down_rows = adapter_down_maps.shape[1] // dataset_size
    down_weight = lax.dynamic_slice_in_dim(
        adapter_down_maps, lax.axis_index("dp") * down_rows, down_rows, 1
    )
    up_columns = adapter_up_maps.shape[2] // dataset_size
    up_weight = lax.dynamic_slice_in_dim(
        adapter_up_maps, lax.axis_index("dp") * up_columns, up_columns, 2
    )
    down_momentum, down_velocity, dir_down = lamb_direction(
        down_weight, down_gradient, down_first_moment, down_second_moment, step_number
    )
    up_momentum, up_velocity, dir_up = lamb_direction(
        up_weight, up_gradient, up_first_moment, up_second_moment, step_number
    )
    sq_down = (
        jnp.stack(
            [jnp.sum(down_weight * down_weight, (1, 2)), jnp.sum(dir_down * dir_down, (1, 2))], 1
        )
        / n_head
    )
    sq_up = jnp.stack([jnp.sum(up_weight * up_weight, (1, 2)), jnp.sum(dir_up * dir_up, (1, 2))], 1)
    total_down, total_up, loss_sum = lax.psum((sq_down, sq_up, loss_part), ("dp", "head"))
    norm_table = jnp.sqrt(jnp.concatenate([total_down, total_up], 0))
    updated_down = (
        down_weight - learn_rate * (norm_table[:2, 0] / norm_table[:2, 1])[:, None, None] * dir_down
    )
    updated_up = (
        up_weight - learn_rate * (norm_table[2:, 0] / norm_table[2:, 1])[:, None, None] * dir_up
    )
    return (
        loss_sum / examples,
        example_norms,
        down_momentum,
        down_velocity,
        updated_down,
        up_momentum,
        up_velocity,
        updated_up,
        norm_table,
    )


def solution(mesh):
    placed = (
        P("dp", None),
        P("dp"),
        P("dp"),
        P(),
        P("dp", "head"),
        P(),
        P(None, None, "head"),
        P("head", None),
        P(None, "head"),
        P("head", None),
        P(),
        P(),
        P(),
        P(),
        P(None, None, "head"),
        P(None, "dp", None),
        P(None, "dp", None),
        P(None, None, ("head", "dp")),
        P(None, None, ("head", "dp")),
        P(None, "dp", None),
        P(None, None, ("head", "dp")),
    )
    return jax.shard_map(
        per_device,
        mesh=mesh,
        in_specs=placed,
        out_specs=(
            P(),
            P(("dp", "head")),
            P(None, "dp", None),
            P(None, "dp", None),
            P(None, "dp", None),
            P(None, None, ("head", "dp")),
            P(None, None, ("head", "dp")),
            P(None, None, ("head", "dp")),
            P(),
        ),
        check_vma=False,
    )
```

profile of v0, /device:TPU:1, one launch (start us, length us, event | category | flops | bytes accessed | tf_op | source)
XLA Modules:
  0.0 1647.0 jit_solution(5846328891770936799)
XLA Ops:
  7.3 19.8 %all_gather.9 = s32[128,512]{1,0:T(8,128)S(1)} all-gather(s32[8,512]{1,0:T(8,128)} %param.22), channel_id=1, replica_groups=mesh['dp'=16,'head'=8] {'dp'}, dimensions={0}, use_global_device_ids=true | all-gather | bytes 278528 | tf_op jit(solution)/shard_map/all_gather | solution.py:277
  28.1 229.0 %gather_fusion = bf16[65536,128]{1,0:T(8,128)(2,1)} fusion(bf16[3144,128]{1,0:T(8,128)(2,1)S(1)} %copy-done.1, s32[65536]{0:T(1024)S(1)} %broadcast_clamp_fusion), kind=kCustom, calls=%fused_computation | custom fusion | bytes 33816576 | tf_op jit(solution)/shard_map/jit(_take)/gather | solution.py:282
  257.0 46.3 %select_convert_fusion = bf16[65536,128]{1,0:T(8,128)(2,1)} fusion(bf16[65536,128]{1,0:T(8,128)(2,1)} %gather_fusion, pred[65536]{0:T(1024)(128)(4,1)S(1)} %compare_and_fusion, pred[65536]{0:T(1024)(128)(4,1)S(1)} %bitcast.555), kind=kLoop, calls=%fused_computation.1 | loop fusion | flops 33554432 | bytes 33685504 | tf_op jit(solution)/shard_map/convert_element_type | solution.py:284
  303.4 115.6 %reduce-scatter.6.cloned.1.call-done = bf16[4096,128]{1,0:T(8,128)(2,1)} async-done(((bf16[65536,128]{1,0:T(8,128)(2,1)}), bf16[4096,128]{1,0:T(8,128)(2,1)}) %reduce-scatter.6.cloned.1.call-update) | async-done | bytes 1048592 | tf_op jit(solution)/shard_map/reduce_scatter | solution.py:283
  423.8 51.6 %all-gather.2.cloned.1.call-done = bf16[4096,1024]{1,0:T(8,128)(2,1)} async-done(((bf16[4096,128]{1,0:T(8,128)(2,1)}), bf16[4096,1024]{1,0:T(8,128)(2,1)}) %all-gather.2.cloned.1.call-update) | async-done | bytes 8388624 | tf_op jit(solution)/shard_map/all_gather | solution.py:294
  475.4 5.1 fusion
  480.5 5.9 multiply_reduce_fusion
  486.4 6.1 multiply_add_fusion
  492.5 3.6 fusion.384
  496.1 4.8 fusion.383
  501.0 3.9 fusion.183
  565.9 3.3 fusion.135
  574.0 3.3 fusion.133
  580.3 183.9 %all-reduce.15.cloned.1.call-done = (f32[1024,1024]{1,0:T(8,128)}, f32[1024,1024]{1,0:T(8,128)}, f32[1024,1024]{1,0:T(8,128)}, f32[1024,1024]{1,0:T(8,128)}) async-done(((f32[1024,1024]{1,0:T(8,128)}, f32[1024,1024]{1,0:T(8,128)}, f32[1024,1024]{1,0:T(8,128)}, f32[1024,1024]{1,0:T(8,128)}), (f32[1024,1024]{1,0:T(8,128)}, f32[1024,1024]{1,0:T(8,128)}, f32[1024,1024]{1,0:T(8,128)}, ...) | async-done | bytes 16777232 | tf_op jit(solution)/shard_map/psum | solution.py:43
  764.3 4.1 fusion.382
  769.0 3.2 copy-done.31
  777.6 6.8 fusion.140
  784.4 6.7 fusion.138
  794.9 6.7 fusion.139
  806.8 6.7 fusion.137
  814.4 183.4 %all-reduce.13.cloned.1.call-done = (f32[1024,1024]{1,0:T(8,128)}, f32[1024,1024]{1,0:T(8,128)}, f32[1024,1024]{1,0:T(8,128)}, f32[1024,1024]{1,0:T(8,128)}) async-done(((f32[1024,1024]{1,0:T(8,128)}, f32[1024,1024]{1,0:T(8,128)}, f32[1024,1024]{1,0:T(8,128)}, f32[1024,1024]{1,0:T(8,128)}), (f32[1024,1024]{1,0:T(8,128)}, f32[1024,1024]{1,0:T(8,128)}, f32[1024,1024]{1,0:T(8,128)}, ...) | async-done | bytes 16777232 | tf_op jit(solution)/shard_map/psum | solution.py:43
  997.8 12.3 fusion.371
  1012.7 4.3 multiply_reduce_fusion.13
  1019.7 5.7 fusion.24
  1027.7 8.9 fusion.18
  1036.7 10.9 fusion.144
  1047.5 3.9 fusion.31
  1051.4 11.0 fusion.143
  1062.5 7.4 fusion.29
  1069.8 10.8 fusion.142
  1080.6 10.9 fusion.141
  1102.5 173.5 %all-reduce.11.cloned.1.call-done = (f32[1024,1024]{1,0:T(8,128)}, f32[1024,1024]{1,0:T(8,128)}, f32[1024,1024]{1,0:T(8,128)}, f32[1024,1024]{1,0:T(8,128)}) async-done(((f32[1024,1024]{1,0:T(8,128)}, f32[1024,1024]{1,0:T(8,128)}, f32[1024,1024]{1,0:T(8,128)}, f32[1024,1024]{1,0:T(8,128)}), (f32[1024,1024]{1,0:T(8,128)}, f32[1024,1024]{1,0:T(8,128)}, f32[1024,1024]{1,0:T(8,128)}, ...) | async-done | bytes 16777232 | tf_op jit(solution)/shard_map/psum | solution.py:146
  1276.0 7.9 fusion.370
  1286.7 3.5 convolution_convert_fusion
  1295.3 5.9 fusion.369
  1304.0 3.5 convolution_convert_fusion.1
  1307.6 3.5 multiply_reduce_fusion.4
  1312.6 5.9 fusion.368
  1321.4 3.5 convolution_convert_fusion.2
  1324.9 3.6 multiply_reduce_fusion.7
  1330.0 5.9 fusion.367
  1338.7 3.5 convolution_convert_fusion.3
  1359.7 29.7 %all-reduce.16 = (bf16[1024,32]{0,1:T(8,128)(2,1)}, bf16[1024,32]{0,1:T(8,128)(2,1)}, bf16[1024,32]{0,1:T(8,128)(2,1)}, bf16[1024,32]{0,1:T(8,128)(2,1)}) all-reduce(f32[1024,32]{0,1:T(8,128)S(1)} %maximum_multiply_fusion.3, f32[1024,32]{0,1:T(8,128)} %maximum_multiply_fusion.2, ...), channel_id=1, replica_groups=mesh['dp'=16,'head'=8] {'head'}, use_global_device_ids=true, to_apply=%region_73.75 | all-reduce | flops 131072 | bytes 786432 | tf_op jit(solution)/shard_map/psum | solution.py:201
  1396.8 10.8 all_to_all.6
  1409.6 12.5 all-reduce
  1426.7 64.2 %reduce-scatter.8.cloned.1.call-done = f32[2,16,8]{1,2,0:T(8,128)} async-done(((f32[2,16,128]{1,2,0:T(8,128)}), f32[2,16,8]{1,2,0:T(8,128)}) %reduce-scatter.8.cloned.1.call-update) | async-done | bytes 1040 | tf_op jit(solution)/shard_map/reduce_scatter | solution.py:331
  1492.3 74.0 %reduce-scatter.10.cloned.1.call-done = f32[64,32]{1,0:T(8,128)} async-done(((f32[1024,32]{1,0:T(8,128)}), f32[64,32]{1,0:T(8,128)}) %reduce-scatter.10.cloned.1.call-update) | async-done | bytes 8208
  1568.7 66.1 %all-reduce.1 = (f32[]{:T(128)}, f32[2,2]{0,1:T(2,128)S(1)}, f32[2,2]{0,1:T(2,128)S(1)}) all-reduce(f32[]{:T(128)S(6)} %div.320, f32[2,2]{0,1:T(2,128)S(1)} %pad_maximum_fusion.2, f32[2,2]{0,1:T(2,128)S(1)} %maximum_multiply_fusion.8), channel_id=1, replica_groups=mesh['dp'=16,'head'=8] {'dp','head'}, use_global_device_ids=true, to_apply=%region_45.47 | all-reduce | flops 9 | bytes 72 | tf_op jit(solution)/shard_map/psum | solution.py:358
  (611 shorter events, 159.5 us)
Async XLA Ops:
  7.2 770.4 %copy-start = (bf16[512,1024]{1,0:T(8,128)(2,1)S(1)}, bf16[512,1024]{1,0:T(8,128)(2,1)}, u32[]{:S(2)}) copy-start(bf16[512,1024]{1,0:T(8,128)(2,1)} %param.31) | copy-start | bytes 3145732
  7.2 20.9 %copy-start.1 = (bf16[3144,128]{1,0:T(8,128)(2,1)S(1)}, bf16[3144,128]{1,0:T(8,128)(2,1)}, u32[]{:S(2)}) copy-start(bf16[3144,128]{1,0:T(8,128)(2,1)} %param.26) | copy-start | bytes 2414596
  7.2 411.8 %reduce-scatter.6.cloned.1.call-start = ((), (), s32[]{:S(2)}) async-start(), calls=%async_computation.4 | async-start | bytes 17825792 | tf_op jit(solution)/shard_map/reduce_scatter | solution.py:283
  303.3 172.0 %all-gather.2.cloned.1.call-start = ((), (), s32[]{:S(2)}) async-start(), calls=%async_computation.5 | async-start | bytes 9437184 | tf_op jit(solution)/shard_map/all_gather | solution.py:294
  419.0 345.2 %all-reduce.15.cloned.1.call-start = ((), (), s32[]{:S(2)}) async-start(), calls=%async_computation.10 | async-start | bytes 33554432 | tf_op jit(solution)/shard_map/psum | solution.py:43
  420.7 151.7 %copy-start.88 = (bf16[2,16,128]{2,1,0:T(8,128)(2,1)}, bf16[2,16,128]{2,1,0:T(8,128)(2,1)S(1)}, u32[]{:S(2)}) copy-start(bf16[2,16,128]{2,1,0:T(8,128)(2,1)S(1)} %convert_element_type.351) | copy-start | bytes 24580
  422.0 151.4 %copy-start.111 = (pred[2,512]{1,0:T(4,128)(4,1)}, pred[2,512]{1,0:T(4,128)(4,1)S(1)}, u32[]{:S(2)}) copy-start(pred[2,512]{1,0:T(4,128)(4,1)S(1)} %get-tuple-element.137) | copy-start | bytes 3076
  500.9 19.8 %copy-start.32 = (f32[2,512,1024]{2,1,0:T(8,128)}, f32[2,512,1024]{2,1,0:T(8,128)S(1)}, u32[]{:S(2)}) copy-start(f32[2,512,1024]{2,1,0:T(8,128)S(1)} %get-tuple-element.79) | copy-start | bytes 12582916
  523.1 14.8 copy-start.71
  524.8 8.6 copy-start.53
  527.2 7.3 copy-start.49
  542.7 15.3 copy-start.69
  544.4 9.1 copy-start.55
  547.3 7.3 copy-start.51
  580.3 417.5 %all-reduce.13.cloned.1.call-start = ((), (), s32[]{:S(2)}) async-start(), calls=%async_computation.9 | async-start | bytes 33554432 | tf_op jit(solution)/shard_map/psum | solution.py:43
  764.3 4.7 copy-start.48
  768.4 5.0 copy-start.26
  777.5 6.8 copy-start.160
  784.4 6.7 copy-start.29
  784.4 6.7 copy-start.47
  794.9 6.7 copy-start.163
  794.9 6.7 copy-start.28
  794.9 6.7 copy-start.46
  813.5 462.4 %all-reduce.11.cloned.1.call-start = ((), (), s32[]{:S(2)}) async-start(), calls=%async_computation.8 | async-start | bytes 33554432 | tf_op jit(solution)/shard_map/psum | solution.py:146
  1010.1 9.6 copy-start.2
  1010.1 9.6 copy-start.6
  1010.1 17.6 %copy-start.4 = (f32[1024,1024]{1,0:T(8,128)}, f32[1024,1024]{1,0:T(8,128)S(1)}, u32[]{:S(2)}) copy-start(f32[1024,1024]{1,0:T(8,128)S(1)} %get-tuple-element.121) | copy-start | bytes 12582916
  1010.1 17.6 %copy-start.8 = (f32[1024,1024]{1,0:T(8,128)}, f32[1024,1024]{1,0:T(8,128)S(1)}, u32[]{:S(2)}) copy-start(f32[1024,1024]{1,0:T(8,128)S(1)} %get-tuple-element.125) | copy-start | bytes 12582916
  1012.7 4.3 copy-start.158
  1091.6 399.3 %reduce-scatter.8.cloned.1.call-start = ((), (), s32[]{:S(2)}) async-start(), calls=%async_computation.6 | async-start | bytes 139264 | tf_op jit(solution)/shard_map/reduce_scatter | solution.py:331
  1275.9 7.9 copy-start.27
  1276.0 7.9 copy-start.45
  1290.2 53.7 %copy-start.78 = (bf16[2,2,64,512]{3,2,1,0:T(8,128)(2,1)}, bf16[2,2,64,512]{3,2,1,0:T(8,128)(2,1)S(1)}, u32[]{:S(2)}) copy-start(bf16[2,2,64,512]{3,2,1,0:T(8,128)(2,1)S(1)} %convolution_convert_fusion) | copy-start | bytes 786436
  1290.2 5.0 copy-start.25
  1307.6 40.5 %copy-start.80 = (bf16[2,2,64,512]{3,2,1,0:T(8,128)(2,1)}, bf16[2,2,64,512]{3,2,1,0:T(8,128)(2,1)S(1)}, u32[]{:S(2)}) copy-start(bf16[2,2,64,512]{3,2,1,0:T(8,128)(2,1)S(1)} %convolution_convert_fusion.1) | copy-start | bytes 786436
  1307.6 5.1 copy-start.23
  1324.9 27.4 %copy-start.82 = (bf16[2,2,64,512]{3,2,1,0:T(8,128)(2,1)}, bf16[2,2,64,512]{3,2,1,0:T(8,128)(2,1)S(1)}, u32[]{:S(2)}) copy-start(bf16[2,2,64,512]{3,2,1,0:T(8,128)(2,1)S(1)} %convolution_convert_fusion.2) | copy-start | bytes 786436
  1324.9 5.1 copy-start.21
  1342.2 13.8 copy-start.84
  1358.9 32.7 %copy-start.38 = (bf16[2,512,1024]{2,1,0:T(8,128)(2,1)S(1)}, bf16[2,512,1024]{2,1,0:T(8,128)(2,1)}, u32[]{:S(2)}) copy-start(bf16[2,512,1024]{2,1,0:T(8,128)(2,1)} %get-tuple-element.84) | copy-start | bytes 6291460
  1423.1 143.2 %reduce-scatter.10.cloned.1.call-start = ((), (), s32[]{:S(2)}) async-start(), calls=%async_computation.7 | async-start | bytes 557056
  1423.2 67.7 %copy-start.122 = (f32[2,16,8]{1,2,0:T(8,128)S(1)}, f32[2,16,8]{1,2,0:T(8,128)}, u32[]{:S(2)}) copy-start(f32[2,16,8]{1,2,0:T(8,128)} %copy.338) | copy-start | bytes 3076
  1423.2 67.7 %copy-start.153 = (f32[2,16,8]{1,2,0:T(8,128)S(1)}, f32[2,16,8]{1,2,0:T(8,128)}, u32[]{:S(2)}) copy-start(f32[2,16,8]{1,2,0:T(8,128)} %param.42) | copy-start | bytes 3076
  1423.2 67.7 %copy-start.154 = (f32[2,16,8]{1,2,0:T(8,128)S(1)}, f32[2,16,8]{1,2,0:T(8,128)}, u32[]{:S(2)}) copy-start(f32[2,16,8]{1,2,0:T(8,128)} %param.40) | copy-start | bytes 3076
  1423.2 67.7 %copy-start.155 = (f32[2,16,8]{1,2,0:T(8,128)S(1)}, f32[2,16,8]{1,2,0:T(8,128)}, u32[]{:S(2)}) copy-start(f32[2,16,8]{1,2,0:T(8,128)} %param.39) | copy-start | bytes 3076
  1424.7 142.5 %copy-start.145 = (f32[2,64,16]{1,2,0:T(8,128)S(1)}, f32[2,64,16]{1,2,0:T(8,128)}, u32[]{:S(2)}) copy-start(f32[2,64,16]{1,2,0:T(8,128)} %param.41) | copy-start | bytes 24580
  1424.7 142.5 %copy-start.146 = (f32[2,64,16]{1,2,0:T(8,128)S(1)}, f32[2,64,16]{1,2,0:T(8,128)}, u32[]{:S(2)}) copy-start(f32[2,64,16]{1,2,0:T(8,128)} %param.38) | copy-start | bytes 24580
  1424.7 142.5 %copy-start.147 = (f32[2,64,16]{1,2,0:T(8,128)S(1)}, f32[2,64,16]{1,2,0:T(8,128)}, u32[]{:S(2)}) copy-start(f32[2,64,16]{1,2,0:T(8,128)} %param.37) | copy-start | bytes 24580
  (123 other events, 271.6 us)
Sparse Core Ops, SparseCore 0:
  303.4 115.5 reduce-scatter.5
  420.7 54.6 all-gather.1
  580.4 183.7 all-reduce.14
  813.6 184.1 all-reduce.12
  1091.7 184.2 all-reduce.10
  1423.2 67.6 reduce-scatter.7
  1494.4 71.8 reduce-scatter.9
where the time goes:
time: 1650 us
  waiting for transfers between devices  846 us (51%)
  local copies, waits for them, and re-layouts  291 us (18%)
  matrix products  177 us (11%)
  other arithmetic  169 us (10%)
  blocking collectives  139 us (8%)
  between operations  24.4 us (1%)
    psum x2, waiting for transfers between devices, branch_add(): total = lax.psum(partial_out, 'head')  367 us
    gather x1, local copies, waits for them, and re-layouts, per_device(): jnp.take(token_embedding_table, jnp.clip(ids_here, 0, vocab_local - 1), a...  229 us
    psum x1, waiting for transfers between devices, layer_forward(): d_one = d_sum_two + lax.psum(back_part, 'head')  173 us
    reduce_scatter x1, waiting for transfers between devices, per_device(): lax.psum_scatter(jnp.where(inside[:, None], picked.astype(jnp.float32), 0...  116 us
    unnamed x8, waiting for transfers between devices  74.1 us
    psum x1, blocking collectives, per_device(): lax.psum((sq_down, sq_up, loss_part), ('dp', 'head'))  66.1 us
    reduce_scatter x1, waiting for transfers between devices, per_device(): lax.psum_scatter(sum_up, 'dp', scatter_dimension=2, tiled=True)  64.2 us
    all_gather x1, waiting for transfers between devices, per_device(): tokens = lax.all_gather(columns, 'head', axis=1, tiled=True)  51.6 us
  transfers between devices with their start and end apart: 7, of which 7 were waited for; matrix products, arithmetic and copies ran while one was open for 1% of the time, Pallas kernels for 0%

commit v1 on v0

--- a/solution.py
+++ b/solution.py
@@ -291,7 +291,9 @@
     down_pair = jnp.concatenate([down_reduced[0], down_reduced[1]], 1)
     micro_examples = ex_dev // MICRO
     own_share = ex_dev // n_head
-    tokens = lax.all_gather(columns, "head", axis=1, tiled=True)
+    tokens = jnp.concatenate(
+        lax.all_to_all(jnp.stack([columns] * lax.axis_size("head")), "head", 0, 0), axis=1
+    )
     hidden_all, unused_std = norm_rows(
         tokens.astype(jnp.float32).reshape(ex_dev, sequence_length, width) + pos_f,
         layer_norm_gains[0],

time: 1650 us -> 1760 us (1.067)
  local copies, waits for them, and re-layouts: 291 us -> 342 us
  waiting for transfers between devices: 846 us -> 871 us
  other arithmetic: 169 us -> 192 us
    all_to_all x0 -> x1, waiting for transfers between devices: none -> 78.6 us  [per_device(): lax.all_to_all(jnp.stack([columns] * lax.axis_size('head')), 'head', 0, 0)]
    all_gather x1 -> x0, waiting for transfers between devices: 51.6 us -> none  [per_device(): tokens = lax.all_gather(columns, 'head', axis=1, tiled=True)]
    convert_element_type x0 -> x2, local copies, waits for them, and re-layouts: none -> 35.9 us  [per_device(): tokens.astype(jnp.float32).reshape(ex_dev, sequence_length, width) + pos_f]
    unnamed x358 -> x363, local copies, waits for them, and re-layouts: 30.4 us -> 38.6 us
    unnamed x8 -> x7, waiting for transfers between devices: 74.1 us -> 74 us
  transfers between devices with their start and end apart: 7 -> 7, of which waited for: 7 -> 7; matrix products, arithmetic and copies ran while one was open for 1% -> 2% of each run, Pallas kernels for 0% -> 0%
where the time goes in v1:
time: 1760 us; the launch traced here: 1750 us
  waiting for transfers between devices  871 us (49%)
  local copies, waits for them, and re-layouts  342 us (19%)
  other arithmetic  192 us (11%)
  matrix products  178 us (10%)
  blocking collectives  139 us (8%)
  between operations  24.5 us (1%)
    psum x2, waiting for transfers between devices, branch_add(): total = lax.psum(partial_out, 'head')  365 us
    gather x1, local copies, waits for them, and re-layouts, per_device(): jnp.take(token_embedding_table, jnp.clip(ids_here, 0, vocab_local - 1), a...  227 us
    psum x1, waiting for transfers between devices, layer_forward(): d_one = d_sum_two + lax.psum(back_part, 'head')  173 us
    reduce_scatter x1, waiting for transfers between devices, per_device(): lax.psum_scatter(jnp.where(inside[:, None], picked.astype(jnp.float32), 0...  116 us
    all_to_all x1, waiting for transfers between devices, per_device(): lax.all_to_all(jnp.stack([columns] * lax.axis_size('head')), 'head', 0, 0)  78.6 us
    unnamed x7, waiting for transfers between devices  74 us
    psum x1, blocking collectives, per_device(): lax.psum((sq_down, sq_up, loss_part), ('dp', 'head'))  66 us
    reduce_scatter x1, waiting for transfers between devices, per_device(): lax.psum_scatter(sum_up, 'dp', scatter_dimension=2, tiled=True)  64.1 us
  transfers between devices with their start and end apart: 7, of which 7 were waited for; matrix products, arithmetic and copies ran while one was open for 2% of the time, Pallas kernels for 0%

profile of v1, /device:TPU:1, one launch (start us, length us, event | category | flops | bytes accessed | tf_op | source)
XLA Modules:
  0.0 1751.0 jit_solution(12820351849052252847)
XLA Ops:
  7.3 19.8 %all_gather.6 = s32[128,512]{1,0:T(8,128)S(1)} all-gather(s32[8,512]{1,0:T(8,128)} %param.22), channel_id=1, replica_groups=mesh['dp'=16,'head'=8] {'dp'}, dimensions={0}, use_global_device_ids=true | all-gather | bytes 278528 | tf_op jit(solution)/shard_map/all_gather | solution.py:277
  28.1 227.3 %gather_fusion = bf16[65536,128]{1,0:T(8,128)(2,1)} fusion(bf16[3144,128]{1,0:T(8,128)(2,1)S(1)} %copy-done.1, s32[65536]{0:T(1024)S(1)} %broadcast_clamp_fusion), kind=kCustom, calls=%fused_computation | custom fusion | bytes 33816576 | tf_op jit(solution)/shard_map/jit(_take)/gather | solution.py:282
  255.3 46.3 %select_convert_fusion = bf16[65536,128]{1,0:T(8,128)(2,1)} fusion(bf16[65536,128]{1,0:T(8,128)(2,1)} %gather_fusion, pred[65536]{0:T(1024)(128)(4,1)S(1)} %compare_and_fusion, pred[65536]{0:T(1024)(128)(4,1)S(1)} %bitcast.558), kind=kLoop, calls=%fused_computation.1 | loop fusion | flops 33554432 | bytes 33685504 | tf_op jit(solution)/shard_map/convert_element_type | solution.py:284
  301.6 115.8 %reduce-scatter.6.cloned.1.call-done = bf16[4096,128]{1,0:T(8,128)(2,1)} async-done(((bf16[65536,128]{1,0:T(8,128)(2,1)}), bf16[4096,128]{1,0:T(8,128)(2,1)}) %reduce-scatter.6.cloned.1.call-update) | async-done | bytes 1048592 | tf_op jit(solution)/shard_map/reduce_scatter | solution.py:283
  417.4 5.5 stack.101
  423.0 5.9 all-to-all-start
  432.7 8.4 copy.348
  444.2 78.6 %all-to-all-done = bf16[8,4096,128]{2,1,0:T(8,128)(2,1)} async-done(((bf16[8,4096,128]{2,1,0:T(8,128)(2,1)}), bf16[8,4096,128]{2,1,0:T(8,128)(2,1)}, u32[]{:S(2)}, u32[]{:S(2)}) %all-to-all-start) | async-done | bytes 8388640 | tf_op jit(solution)/shard_map/all_to_all | solution.py:295
  522.8 10.3 convert_bitcast_fusion
  533.1 17.9 %copy.180 = f32[4096,8,128]{2,1,0:T(8,128)} copy(f32[4096,8,128]{2,0,1:T(8,128)} %convert_bitcast_fusion) | data formatting | bytes 33554432 | tf_op jit(solution)/shard_map/convert_element_type | solution.py:298
  550.9 18.0 %reshape.664 = f32[8,512,1024]{2,1,0:T(8,128)} reshape(f32[4096,8,128]{2,1,0:T(8,128)} %copy.180) | data formatting | bytes 33554432 | tf_op jit(solution)/shard_map/convert_element_type | solution.py:298
  569.0 11.1 fusion
  580.1 11.3 multiply_reduce_fusion
  591.5 7.6 multiply_add_fusion
  599.1 3.6 fusion.384
  602.7 5.1 fusion.383
  607.8 3.9 fusion.183
  687.1 181.4 %all-reduce.15.cloned.1.call-done = (f32[1024,1024]{1,0:T(8,128)}, f32[1024,1024]{1,0:T(8,128)}, f32[1024,1024]{1,0:T(8,128)}, f32[1024,1024]{1,0:T(8,128)}) async-done(((f32[1024,1024]{1,0:T(8,128)}, f32[1024,1024]{1,0:T(8,128)}, f32[1024,1024]{1,0:T(8,128)}, f32[1024,1024]{1,0:T(8,128)}), (f32[1024,1024]{1,0:T(8,128)}, f32[1024,1024]{1,0:T(8,128)}, f32[1024,1024]{1,0:T(8,128)}, ...) | async-done | bytes 16777232 | tf_op jit(solution)/shard_map/psum | solution.py:43
  868.4 4.1 fusion.382
  881.7 6.9 fusion.140
  888.6 6.7 fusion.138
  899.2 6.7 fusion.139
  911.0 6.7 fusion.137
  918.6 183.4 %all-reduce.13.cloned.1.call-done = (f32[1024,1024]{1,0:T(8,128)}, f32[1024,1024]{1,0:T(8,128)}, f32[1024,1024]{1,0:T(8,128)}, f32[1024,1024]{1,0:T(8,128)}) async-done(((f32[1024,1024]{1,0:T(8,128)}, f32[1024,1024]{1,0:T(8,128)}, f32[1024,1024]{1,0:T(8,128)}, f32[1024,1024]{1,0:T(8,128)}), (f32[1024,1024]{1,0:T(8,128)}, f32[1024,1024]{1,0:T(8,128)}, f32[1024,1024]{1,0:T(8,128)}, ...) | async-done | bytes 16777232 | tf_op jit(solution)/shard_map/psum | solution.py:43
  1102.0 12.5 fusion.371
  1117.1 4.3 multiply_reduce_fusion.13
  1124.1 5.7 fusion.24
  1132.1 8.7 fusion.18
  1140.8 10.9 fusion.144
  1151.7 3.9 fusion.31
  1155.6 11.0 fusion.143
  1166.7 7.3 fusion.29
  1174.0 11.0 fusion.142
  1185.1 10.9 fusion.141
  1206.9 173.4 %all-reduce.11.cloned.1.call-done = (f32[1024,1024]{1,0:T(8,128)}, f32[1024,1024]{1,0:T(8,128)}, f32[1024,1024]{1,0:T(8,128)}, f32[1024,1024]{1,0:T(8,128)}) async-done(((f32[1024,1024]{1,0:T(8,128)}, f32[1024,1024]{1,0:T(8,128)}, f32[1024,1024]{1,0:T(8,128)}, f32[1024,1024]{1,0:T(8,128)}), (f32[1024,1024]{1,0:T(8,128)}, f32[1024,1024]{1,0:T(8,128)}, f32[1024,1024]{1,0:T(8,128)}, ...) | async-done | bytes 16777232 | tf_op jit(solution)/shard_map/psum | solution.py:146
  1380.3 7.6 fusion.370
  1399.4 5.9 fusion.369
  1411.7 3.5 multiply_reduce_fusion.4
  1416.7 5.9 fusion.368
  1425.5 3.5 convolution_convert_fusion.2
  1429.0 3.7 multiply_reduce_fusion.7
  1434.1 5.9 fusion.367
  1463.9 29.8 %all-reduce.16 = (bf16[1024,32]{0,1:T(8,128)(2,1)}, bf16[1024,32]{0,1:T(8,128)(2,1)}, bf16[1024,32]{0,1:T(8,128)(2,1)}, bf16[1024,32]{0,1:T(8,128)(2,1)}) all-reduce(f32[1024,32]{0,1:T(8,128)S(1)} %maximum_multiply_fusion.3, f32[1024,32]{0,1:T(8,128)} %maximum_multiply_fusion.2, ...), channel_id=1, replica_groups=mesh['dp'=16,'head'=8] {'head'}, use_global_device_ids=true, to_apply=%region_73.75 | all-reduce | flops 131072 | bytes 786432 | tf_op jit(solution)/shard_map/psum | solution.py:201
  1500.9 10.8 all_to_all.11
  1513.8 12.5 all-reduce
  1530.9 64.1 %reduce-scatter.8.cloned.1.call-done = f32[2,16,8]{1,2,0:T(8,128)} async-done(((f32[2,16,128]{1,2,0:T(8,128)}), f32[2,16,8]{1,2,0:T(8,128)}) %reduce-scatter.8.cloned.1.call-update) | async-done | bytes 1040 | tf_op jit(solution)/shard_map/reduce_scatter | solution.py:333
  1596.4 73.9 %reduce-scatter.10.cloned.1.call-done = f32[64,32]{1,0:T(8,128)} async-done(((f32[1024,32]{1,0:T(8,128)}), f32[64,32]{1,0:T(8,128)}) %reduce-scatter.10.cloned.1.call-update) | async-done | bytes 8208
  1672.7 66.0 %all-reduce.1 = (f32[]{:T(128)}, f32[2,2]{0,1:T(2,128)S(1)}, f32[2,2]{0,1:T(2,128)S(1)}) all-reduce(f32[]{:T(128)S(6)} %div.320, f32[2,2]{0,1:T(2,128)S(1)} %pad_maximum_fusion.2, f32[2,2]{0,1:T(2,128)S(1)} %maximum_multiply_fusion.8), channel_id=1, replica_groups=mesh['dp'=16,'head'=8] {'dp','head'}, use_global_device_ids=true, to_apply=%region_45.47 | all-reduce | flops 9 | bytes 72 | tf_op jit(solution)/shard_map/psum | solution.py:360
  (620 shorter events, 181.9 us)
Async XLA Ops:
  7.2 874.5 %copy-start = (bf16[512,1024]{1,0:T(8,128)(2,1)S(1)}, bf16[512,1024]{1,0:T(8,128)(2,1)}, u32[]{:S(2)}) copy-start(bf16[512,1024]{1,0:T(8,128)(2,1)} %param.31) | copy-start | bytes 3145732
  7.2 20.9 %copy-start.1 = (bf16[3144,128]{1,0:T(8,128)(2,1)S(1)}, bf16[3144,128]{1,0:T(8,128)(2,1)}, u32[]{:S(2)}) copy-start(bf16[3144,128]{1,0:T(8,128)(2,1)} %param.26) | copy-start | bytes 2414596
  7.2 410.2 %reduce-scatter.6.cloned.1.call-start = ((), (), s32[]{:S(2)}) async-start(), calls=%async_computation.5 | async-start | bytes 17825792 | tf_op jit(solution)/shard_map/reduce_scatter | solution.py:283
  423.0 99.8 %all-to-all-start = ((bf16[8,4096,128]{2,1,0:T(8,128)(2,1)}), bf16[8,4096,128]{2,1,0:T(8,128)(2,1)}, u32[]{:S(2)}, u32[]{:S(2)}) async-start(bf16[8,4096,128]{2,1,0:T(8,128)(2,1)} %stack.101), calls=%async_computation.1 | async-start | bytes 16777216 | tf_op jit(solution)/shard_map/all_to_all | solution.py:295
  428.9 439.5 %all-reduce.15.cloned.1.call-start = ((), (), s32[]{:S(2)}) async-start(), calls=%async_computation.10 | async-start | bytes 33554432 | tf_op jit(solution)/shard_map/psum | solution.py:43
  432.6 8.4 copy-start.104
  432.6 8.4 copy-start.139
  432.7 8.4 copy-start.150
  432.7 9.7 copy-start.152
  432.7 10.3 copy-start.153
  441.1 238.0 %copy-start.90 = (bf16[2,16,128]{2,1,0:T(8,128)(2,1)}, bf16[2,16,128]{2,1,0:T(8,128)(2,1)S(1)}, u32[]{:S(2)}) copy-start(bf16[2,16,128]{2,1,0:T(8,128)(2,1)S(1)} %convert_element_type.366) | copy-start | bytes 24580
  442.4 237.6 %copy-start.113 = (pred[2,512]{1,0:T(4,128)(4,1)}, pred[2,512]{1,0:T(4,128)(4,1)S(1)}, u32[]{:S(2)}) copy-start(pred[2,512]{1,0:T(4,128)(4,1)S(1)} %get-tuple-element.137) | copy-start | bytes 3076
  580.1 11.4 copy-start.43
  607.8 19.8 %copy-start.32 = (f32[2,512,1024]{2,1,0:T(8,128)}, f32[2,512,1024]{2,1,0:T(8,128)S(1)}, u32[]{:S(2)}) copy-start(f32[2,512,1024]{2,1,0:T(8,128)S(1)} %get-tuple-element.79) | copy-start | bytes 12582916
  630.0 14.6 copy-start.73
  631.7 8.3 copy-start.55
  633.8 7.3 copy-start.51
  649.4 15.2 copy-start.71
  651.1 9.1 copy-start.57
  654.0 7.3 copy-start.53
  687.0 415.0 %all-reduce.13.cloned.1.call-start = ((), (), s32[]{:S(2)}) async-start(), calls=%async_computation.9 | async-start | bytes 33554432 | tf_op jit(solution)/shard_map/psum | solution.py:43
  881.7 6.9 copy-start.162
  888.6 6.7 copy-start.29
  888.6 6.7 copy-start.49
  899.1 6.7 copy-start.165
  899.1 6.7 copy-start.28
  899.2 6.7 copy-start.48
  917.7 462.6 %all-reduce.11.cloned.1.call-start = ((), (), s32[]{:S(2)}) async-start(), calls=%async_computation.8 | async-start | bytes 33554432 | tf_op jit(solution)/shard_map/psum | solution.py:146
  1114.5 9.6 copy-start.2
  1114.5 9.6 copy-start.6
  1114.5 17.6 %copy-start.4 = (f32[1024,1024]{1,0:T(8,128)}, f32[1024,1024]{1,0:T(8,128)S(1)}, u32[]{:S(2)}) copy-start(f32[1024,1024]{1,0:T(8,128)S(1)} %get-tuple-element.121) | copy-start | bytes 12582916
  1114.5 17.6 %copy-start.8 = (f32[1024,1024]{1,0:T(8,128)}, f32[1024,1024]{1,0:T(8,128)S(1)}, u32[]{:S(2)}) copy-start(f32[1024,1024]{1,0:T(8,128)S(1)} %get-tuple-element.125) | copy-start | bytes 12582916
  1196.0 399.0 %reduce-scatter.8.cloned.1.call-start = ((), (), s32[]{:S(2)}) async-start(), calls=%async_computation.6 | async-start | bytes 139264 | tf_op jit(solution)/shard_map/reduce_scatter | solution.py:333
  1380.3 7.6 copy-start.27
  1380.3 7.6 copy-start.47
  1394.3 53.7 %copy-start.80 = (bf16[2,2,64,512]{3,2,1,0:T(8,128)(2,1)}, bf16[2,2,64,512]{3,2,1,0:T(8,128)(2,1)S(1)}, u32[]{:S(2)}) copy-start(bf16[2,2,64,512]{3,2,1,0:T(8,128)(2,1)S(1)} %convolution_convert_fusion) | copy-start | bytes 786436
  1411.6 40.5 %copy-start.82 = (bf16[2,2,64,512]{3,2,1,0:T(8,128)(2,1)}, bf16[2,2,64,512]{3,2,1,0:T(8,128)(2,1)S(1)}, u32[]{:S(2)}) copy-start(bf16[2,2,64,512]{3,2,1,0:T(8,128)(2,1)S(1)} %convolution_convert_fusion.1) | copy-start | bytes 786436
  1429.0 27.4 %copy-start.84 = (bf16[2,2,64,512]{3,2,1,0:T(8,128)(2,1)}, bf16[2,2,64,512]{3,2,1,0:T(8,128)(2,1)S(1)}, u32[]{:S(2)}) copy-start(bf16[2,2,64,512]{3,2,1,0:T(8,128)(2,1)S(1)} %convolution_convert_fusion.2) | copy-start | bytes 786436
  1446.3 13.8 copy-start.86
  1463.0 32.8 %copy-start.38 = (bf16[2,512,1024]{2,1,0:T(8,128)(2,1)S(1)}, bf16[2,512,1024]{2,1,0:T(8,128)(2,1)}, u32[]{:S(2)}) copy-start(bf16[2,512,1024]{2,1,0:T(8,128)(2,1)} %get-tuple-element.84) | copy-start | bytes 6291460
  1527.3 143.0 %reduce-scatter.10.cloned.1.call-start = ((), (), s32[]{:S(2)}) async-start(), calls=%async_computation.7 | async-start | bytes 557056
  1527.3 67.7 %copy-start.124 = (f32[2,16,8]{1,2,0:T(8,128)S(1)}, f32[2,16,8]{1,2,0:T(8,128)}, u32[]{:S(2)}) copy-start(f32[2,16,8]{1,2,0:T(8,128)} %copy.340) | copy-start | bytes 3076
  1527.3 67.7 %copy-start.155 = (f32[2,16,8]{1,2,0:T(8,128)S(1)}, f32[2,16,8]{1,2,0:T(8,128)}, u32[]{:S(2)}) copy-start(f32[2,16,8]{1,2,0:T(8,128)} %param.42) | copy-start | bytes 3076
  1527.4 67.7 %copy-start.156 = (f32[2,16,8]{1,2,0:T(8,128)S(1)}, f32[2,16,8]{1,2,0:T(8,128)}, u32[]{:S(2)}) copy-start(f32[2,16,8]{1,2,0:T(8,128)} %param.40) | copy-start | bytes 3076
  1527.4 67.7 %copy-start.157 = (f32[2,16,8]{1,2,0:T(8,128)S(1)}, f32[2,16,8]{1,2,0:T(8,128)}, u32[]{:S(2)}) copy-start(f32[2,16,8]{1,2,0:T(8,128)} %param.39) | copy-start | bytes 3076
  1528.9 142.4 %copy-start.147 = (f32[2,64,16]{1,2,0:T(8,128)S(1)}, f32[2,64,16]{1,2,0:T(8,128)}, u32[]{:S(2)}) copy-start(f32[2,64,16]{1,2,0:T(8,128)} %param.41) | copy-start | bytes 24580
  1528.9 142.4 %copy-start.148 = (f32[2,64,16]{1,2,0:T(8,128)S(1)}, f32[2,64,16]{1,2,0:T(8,128)}, u32[]{:S(2)}) copy-start(f32[2,64,16]{1,2,0:T(8,128)} %param.38) | copy-start | bytes 24580
  1528.9 142.3 %copy-start.149 = (f32[2,64,16]{1,2,0:T(8,128)S(1)}, f32[2,64,16]{1,2,0:T(8,128)}, u32[]{:S(2)}) copy-start(f32[2,64,16]{1,2,0:T(8,128)} %param.37) | copy-start | bytes 24580
  (125 other events, 295.3 us)
Sparse Core Ops, SparseCore 0:
  301.7 115.6 reduce-scatter.5
  687.1 181.2 all-reduce.14
  917.9 184.1 all-reduce.12
  1196.1 184.1 all-reduce.10
  1527.4 67.5 reduce-scatter.7
  1598.4 71.8 reduce-scatter.9
